TPU v7x, 128 devices: a whole 4x4x4 slice. The times are simulated.
128 devices in a mesh: seq: 8 (over y, x_hi), rep: 16 (over x_lo, z, core).
Axes of the slice: x: 4 (x_hi: 2, x_lo: 2; x = x_hi * 2 + x_lo), y: 4, z: 4, core: 2. Of those that a mesh axis runs over, the one named last changes fastest.
Arguments:
- tile_embed: bfloat16 [16, 8192, 768], P('rep', 'seq'), may hold values from -6 to 6
- tile_source: int32 [16, 8192], P('rep', 'seq'), may hold values from 0 to 8191, as said below
- slide_len: int32 [16], P('rep'), may hold values from 4096 to 8192
- grad_out: bfloat16 [16, 8192, 768], P('rep', 'seq'), may hold values from -6 to 6
- w_query: bfloat16 [768, 768], replicated, may hold values from -0.11727427342914273 to 0.11727427342914273
- w_key: bfloat16 [768, 768], replicated, may hold values from -0.11727427342914273 to 0.11727427342914273
- w_value: bfloat16 [768, 768], replicated, may hold values from -0.21875 to 0.21875
- w_out: bfloat16 [768, 768], replicated, may hold values from -0.21875 to 0.21875
Outputs:
- encoded: bfloat16 [16, 8192, 768], P('rep', 'seq')
- embed_grad: bfloat16 [16, 8192, 768], P('rep', 'seq')
- grad_query: float32 [768, 768], replicated
- grad_key: float32 [768, 768], replicated
- grad_value: float32 [768, 768], replicated
- grad_outproj: float32 [768, 768], replicated
Inputs may be any that keep to these rules, and one draw needn't show every extreme that they name: For each slide, tile_source is a permutation of 0 to 8191; each run of 1024 slide positions (aligned) takes exactly 1024 // (number of such runs) rows from each aligned run of 1024 rows of tile_embed.
All inputs are finite; a program needn't handle non-finite values.
Results may differ from a plain program's by a relative error of at most 0.0025.
The roundings to bfloat16 on the way count: a program that leaves them out, or rounds other values in their place, can miss the bound.
Values may be sent and summed in bfloat16 or wider, within the bound.
A program may use at most 192 MiB of HBM per device.

v0:
```python
import jax
import jax.numpy as jnp
from jax import lax
from jax.sharding import PartitionSpec as P

HEADS = 16
SEG = 1024
RATE = 16
NEGATIVE = -1e30


def sent_together(arrays, axis, dim, along):
    both = jnp.concatenate(arrays, axis=along)
    result, at, done = (lax.all_gather(both, axis, axis=dim, tiled=True), 0, [])
    for a in arrays:
        done.append(lax.slice_in_dim(result, at, at + a.shape[along], axis=along))
        at += a.shape[along]
    return tuple(done)


def side_by_side(arrays, axis, dim, along):
    widths = [a.shape[along] for a in arrays]
    both = jnp.concatenate(arrays, axis=along)
    result = lax.psum_scatter(both, axis, scatter_dimension=dim, tiled=True)
    return tuple(jnp.split(result, [sum(widths[:k]) for k in range(1, len(widths))], axis=along))


def chosen(dilation, head_count):
    return jnp.arange(dilation)[:, None] == (jnp.arange(head_count) % dilation)[None, :]


def sparse_rows(dense, dilation):
    row_count, head_count, trailing = dense.shape
    blocks = dense.astype(jnp.float32).reshape(
        row_count // dilation, dilation, head_count, trailing
    )
    selected = chosen(dilation, head_count)[None, :, :, None]
    return jnp.sum(jnp.where(selected, blocks, jnp.float32(0.0)), axis=1)


def spread_rows(sparse, dilation, filler):
    row_count, head_count, trailing = sparse.shape
    selected = chosen(dilation, head_count)[None, :, :, None]
    spread = jnp.where(selected, sparse[:, None], jnp.float32(filler))
    return spread.reshape(row_count * dilation, head_count, trailing)


def product(pattern, left_side, right_side):
    return jnp.einsum(pattern, left_side, right_side, preferred_element_type=jnp.float32)


def masked_scores(queries, key_rows, key_ok, pieces, scaling):
    scores = product("nqd,nkd->nqk", queries, key_rows) * scaling
    return jnp.where(key_ok.reshape(pieces, 1, -1), scores, NEGATIVE)


def head_forward(queries, key_rows, values, key_ok, pieces, scaling):
    head_width = queries.shape[-1]
    queries = queries.reshape(pieces, -1, head_width)
    key_rows = key_rows.reshape(pieces, -1, head_width)
    values = values.reshape(pieces, -1, head_width)
    scores = masked_scores(queries, key_rows, key_ok, pieces, scaling)
    maxima = jnp.max(scores, axis=-1)
    weights = jnp.exp(scores - maxima[..., None])
    totals = jnp.sum(weights, axis=-1)
    numerator = product("nqk,nkd->nqd", weights.astype(jnp.bfloat16), values)
    return (numerator.reshape(-1, head_width), maxima.reshape(-1), totals.reshape(-1))


def split_pieces(arrays, pieces):
    return tuple((member.reshape(pieces, -1, member.shape[-1]) for member in arrays))


def score_terms(queries, key_rows, values, key_ok, log_total, upstream, deltas, pieces, scaling):
    scores = masked_scores(queries, key_rows, key_ok, pieces, scaling)
    probabilities = jnp.exp(scores - log_total.reshape(pieces, -1, 1))
    prob_grad = product("nqd,nkd->nqk", upstream, values)
    score_grad = (probabilities * (prob_grad - deltas.reshape(pieces, -1, 1))).astype(jnp.bfloat16)
    return (probabilities, score_grad)


def head_backward(queries, key_rows, values, key_ok, log_total, upstream, deltas, pieces, scaling):
    head_width = queries.shape[-1]
    queries, key_rows, values, upstream = split_pieces(
        (queries, key_rows, values, upstream), pieces
    )
    probabilities, score_grad = score_terms(
        queries, key_rows, values, key_ok, log_total, upstream, deltas, pieces, scaling
    )
    value_grad = product("nqk,nqd->nkd", probabilities.astype(jnp.bfloat16), upstream)
    query_grad = product("nqk,nkd->nqd", score_grad, key_rows) * scaling
    key_grad = product("nqk,nqd->nkd", score_grad, queries) * scaling
    return (
        query_grad.reshape(-1, head_width),
        key_grad.reshape(-1, head_width),
        value_grad.reshape(-1, head_width),
    )


def heads_map(function, arrays, pieces, scaling):
    transposed = tuple((jnp.moveaxis(member, 1, 0) for member in arrays))
    results = lax.map(lambda members: function(*members, pieces, scaling), transposed)
    return tuple((jnp.moveaxis(member, 0, 1) for member in results))


def merge_parts(local_part, remote, dilation):
    numer_local, max_local, total_local = local_part
    numer_far = spread_rows(remote[0], dilation, 0.0)
    max_far = spread_rows(remote[1][..., None], dilation, NEGATIVE)[..., 0]
    total_far = spread_rows(remote[2][..., None], dilation, 0.0)[..., 0]
    highest = jnp.maximum(max_local, max_far)
    weight_local = jnp.exp(max_local - highest)
    weight_far = jnp.exp(max_far - highest)
    combined = total_local * weight_local + total_far * weight_far
    output = (numer_local * weight_local[..., None] + numer_far * weight_far[..., None]) / combined[
        ..., None
    ]
    return (output, highest + jnp.log(combined))


def project(left_side, right_side):
    return jnp.dot(left_side, right_side, preferred_element_type=jnp.float32)


def per_device(tile_embed, tile_source, slide_len, grad_out, w_query, w_key, w_value, w_out):
    owned_rows = tile_embed[0]
    source = tile_source[0]
    row_count, features = owned_rows.shape
    stripes = lax.axis_size("seq")
    stripe = lax.axis_index("seq")
    portion = row_count // stripes
    owner_dev = source // row_count
    ordering = jnp.argsort(owner_dev, stable=True)
    wanted = (source % row_count)[ordering].reshape(stripes, portion)
    requested = lax.all_to_all(wanted, "seq", split_axis=0, concat_axis=0, tiled=True)
    picked = jnp.take(owned_rows, requested.reshape(-1), axis=0).reshape(stripes, portion, features)
    arrived = lax.all_to_all(picked, "seq", split_axis=0, concat_axis=0, tiled=True).reshape(
        row_count, features
    )
    embedded = jnp.zeros_like(arrived).at[ordering].set(arrived)
    length = slide_len[0]
    upstream_in = grad_out[0]
    head_dim = features // HEADS
    scaling = head_dim ** (-0.5)
    positions = stripe * row_count + jnp.arange(row_count)
    valid_rows = positions < length
    queries = project(embedded, w_query).astype(jnp.bfloat16).reshape(row_count, HEADS, head_dim)
    key_rows = project(embedded, w_key).astype(jnp.bfloat16).reshape(row_count, HEADS, head_dim)
    values = project(embedded, w_value).astype(jnp.bfloat16).reshape(row_count, HEADS, head_dim)
    local_ok = jnp.broadcast_to(valid_rows[:, None], (row_count, HEADS))
    local_part = heads_map(
        head_forward, (queries, key_rows, values, local_ok), row_count // SEG, scaling
    )
    sparse_q = sparse_rows(queries, RATE).astype(jnp.bfloat16)
    sparse_k = sparse_rows(key_rows, RATE).astype(jnp.bfloat16)
    sparse_v = sparse_rows(values, RATE).astype(jnp.bfloat16)
    near_count = sparse_k.shape[0]
    far_k, far_v = sent_together(
        (sparse_k.reshape(near_count, features), sparse_v.reshape(near_count, features)),
        "seq",
        0,
        1,
    )
    far_count = far_k.shape[0]
    far_k = far_k.reshape(far_count, HEADS, head_dim)
    far_v = far_v.reshape(far_count, HEADS, head_dim)
    sparse_pos = jnp.arange(far_count)[:, None] * RATE + (jnp.arange(HEADS) % RATE)[None, :]
    sparse_ok = sparse_pos < length
    remote = heads_map(head_forward, (sparse_q, far_k, far_v, sparse_ok), 1, scaling)
    output, log_total = merge_parts(local_part, remote, RATE)
    attended = (
        (output * valid_rows[:, None, None]).astype(jnp.bfloat16).reshape(row_count, features)
    )
    encoded = (embedded.astype(jnp.float32) + project(attended, w_out)).astype(jnp.bfloat16)
    upstream = (
        (project(upstream_in, w_out.T) * valid_rows[:, None])
        .astype(jnp.bfloat16)
        .reshape(row_count, HEADS, head_dim)
    )
    deltas = jnp.sum(upstream.astype(jnp.float32) * output, axis=-1)
    grad_outproj = jnp.einsum(
        "td,te->de", attended, upstream_in, preferred_element_type=jnp.float32
    )
    local_grads = heads_map(
        head_backward,
        (queries, key_rows, values, local_ok, log_total, upstream, deltas),
        row_count // SEG,
        scaling,
    )
    sparse_up = sparse_rows(upstream, RATE).astype(jnp.bfloat16)
    sparse_delta = sparse_rows(deltas[..., None], RATE)[..., 0]
    sparse_total = sparse_rows(log_total[..., None], RATE)[..., 0]
    remote_grads = heads_map(
        head_backward,
        (sparse_q, far_k, far_v, sparse_ok, sparse_total, sparse_up, sparse_delta),
        1,
        scaling,
    )
    key_back, value_back = side_by_side(
        (
            remote_grads[1].reshape(far_count, features),
            remote_grads[2].reshape(far_count, features),
        ),
        "seq",
        0,
        1,
    )
    key_back = key_back.reshape(near_count, HEADS, head_dim)
    value_back = value_back.reshape(near_count, HEADS, head_dim)
    query_far = remote_grads[0]
    query_grad = (
        (local_grads[0] + spread_rows(query_far, RATE, 0.0))
        .astype(jnp.bfloat16)
        .reshape(row_count, features)
    )
    key_grad = (
        (local_grads[1] + spread_rows(key_back, RATE, 0.0))
        .astype(jnp.bfloat16)
        .reshape(row_count, features)
    )
    value_grad = (
        (local_grads[2] + spread_rows(value_back, RATE, 0.0))
        .astype(jnp.bfloat16)
        .reshape(row_count, features)
    )
    embed_grad = upstream_in.astype(jnp.float32) + project(query_grad, w_query.T)
    embed_grad = embed_grad + project(key_grad, w_key.T)
    embed_grad = (embed_grad + project(value_grad, w_value.T)).astype(jnp.bfloat16)
    grad_query = jnp.einsum("td,te->de", embedded, query_grad, preferred_element_type=jnp.float32)
    grad_key = jnp.einsum("td,te->de", embedded, key_grad, preferred_element_type=jnp.float32)
    grad_value = jnp.einsum("td,te->de", embedded, value_grad, preferred_element_type=jnp.float32)
    summed = lax.psum((grad_query, grad_key, grad_value, grad_outproj), ("seq", "rep"))
    return (encoded[None], embed_grad[None], summed[0], summed[1], summed[2], summed[3])


def solution(mesh):
    return jax.shard_map(
        per_device,
        mesh=mesh,
        in_specs=(
            P("rep", "seq", None),
            P("rep", "seq"),
            P("rep"),
            P("rep", "seq", None),
            P(),
            P(),
            P(),
            P(),
        ),
        out_specs=(P("rep", "seq", None), P("rep", "seq", None), P(), P(), P(), P()),
        check_vma=False,
    )
```

profile of v0, /device:TPU:1, one launch (start us, length us, event | category | flops | bytes accessed | tf_op | source)
XLA Modules:
  0.0 927.7 jit_solution(13894790200978015584)
XLA Ops:
  12.4 4.5 gather_fusion
  16.9 13.8 %all_to_all.14 = s32[8,1,128]{2,1,0:T(1,128)S(1)} all-to-all(s32[8,1,128]{2,1,0:T(1,128)S(1)} %bitcast.386), channel_id=1, replica_groups=mesh['seq'=8,'rep'=16] {'seq'}, dimensions={0} | all-to-all | bytes 8192 | tf_op jit(solution)/shard_map/all_to_all | solution.py:135
  47.3 4.8 copy.100
  55.3 7.8 reshape.434
  65.1 6.4 scatter_custom_fusion
  76.8 7.8 reshape.431
  90.0 7.8 reshape.432
  105.1 7.8 reshape.433
  112.9 14.1 %select_reduce_fusion = (bf16[64,16,48]{2,1,0:T(8,128)(2,1)S(1)}, bf16[64,16,48]{2,1,0:T(8,128)(2,1)}, bf16[64,16,48]{2,1,0:T(8,128)(2,1)}, bf16[64,16,48]{2,1,0:T(8,128)(2,1)}) fusion(f32[64,16,16,48]{3,2,1,0:T(8,128)} %reshape.434, pred[16,16]{1,0:T(8,128)(4,1)} %copy-done.23, f32[64,16,16,48]{3,2,1,0:T(8,128)} %reshape.432, ...), kind=kLoop, calls=%fused_computation.133 | loop fusion | flops 6094848 | bytes 12976384 | tf_op jit(solution)/shard_map/reduce_sum | solution.py:38
  144.3 142.6 %while.56 = (s32[]{:T(128)}, f32[16,1024,48]{1,2,0:T(8,128)}, f32[16,1024]{1,0:T(8,128)S(1)}, f32[16,1024]{1,0:T(8,128)S(1)}, pred[16,1024]{1,0:T(8,128)(4,1)S(1...) while((s32[]{:T(128)}, f32[16,1024,48]{1,2,0:T(8,128)}, ...), condition=%wide.region_5.6_spmd, body=%wide.region_2.5_spmd.sunk | while | flops 212858880 | bytes 30383244 | solution.py:102
  287.0 7.9 copy.83
  301.3 42.2 %while.57 = (s32[]{:T(128)}, f32[16,64,48]{1,2,0:T(8,128)S(1)}, f32[16,64]{1,0:T(8,128)S(1)}, f32[16,64]{1,0:T(8,128)S(1)}, pred[16,512]{1,0:T(8,128)(4,1)S(1)},...) while((s32[]{:T(128)}, f32[16,64,48]{1,2,0:T(8,128)S(1)}, ...), condition=%wide.region_12.13_spmd, body=%wide.region_9.12_spmd.sunk | while | flops 6520706 | bytes 702321 | solution.py:102
  346.2 13.4 %multiply_convert_fusion.1 = (bf16[1024,16,48]{2,1,0:T(8,128)(2,1)}, f32[1024,16,48]{2,1,0:T(8,128)S(1)}) fusion(f32[1024]{0:T(1024)S(1)} %copy-done.25, f32[1024,16]{1,0:T(8,128)} %copy.97, f32[1024,16]{1,0:T(8,128)S(1)} %copy.96, f32[64,16,48]{2,1,0:T(8,128)S(1)} %copy.95, pred[1024,16]{1,0:T(8,128)(4,1)S(1)} %copy.94, f32[1024,16]{1,0:T(8,128)S(1)} %copy.93, ...), kind=kLoop, calls=%fused_computation.135 | loop fusion | flops 5505024 | bytes 8278016 | tf_op jit(solution)/shard_map/convert_element_type | solution.py:172
  362.9 103.9 %while.59 = (s32[]{:T(128)}, f32[16,64,48]{1,2,0:T(8,128)S(1)}, f32[16,512,48]{1,2,0:T(8,128)}, f32[16,512,48]{1,2,0:T(8,128)}, pred[16,512]{1,0:T(8,128)(4,1)S(...) while((s32[]{:T(128)}, f32[16,64,48]{1,2,0:T(8,128)S(1)}, ...), condition=%wide.region_20.21_spmd, body=%wide.region_19.20_spmd.sunk | while | flops 15985666 | bytes 1278077 | solution.py:102
  481.0 181.1 %while.58 = (s32[]{:T(128)}, f32[16,1024,48]{1,2,0:T(8,128)}, f32[16,1024,48]{1,2,0:T(8,128)}, f32[16,1024,48]{1,2,0:T(8,128)}, pred[16,1024]{1,0:T(8,128)(4,1)S...) while((s32[]{:T(128)}, f32[16,1024,48]{1,2,0:T(8,128)}, ...), condition=%wide.region_15.16_spmd, body=%wide.region_14.15_spmd.sunk | while | flops 513900544 | bytes 21337212 | solution.py:102
  662.5 7.9 copy.102
  670.3 7.8 copy.112
  678.2 7.8 copy.115
  686.0 5.5 copy.98
  699.3 15.1 %fusion.110 = (bf16[1024,16,48]{2,1,0:T(8,128)(2,1)}, bf16[1024,16,48]{2,1,0:T(8,128)(2,1)}, bf16[1024,16,48]{2,1,0:T(8,128)(2,1)}) fusion(f32[16,1024,48]{2,0,1:T(8,128)} %copy.102, f32[64,16,48]{2,1,0:T(8,128)S(1)} %copy.110, pred[1024,16]{1,0:T(8,128)(4,1)} %copy-done.14, f32[64,16,48]{2,1,0:T(8,128)S(1)} %copy.113, f32[16,1024,48]{2,0,1:T(8,128)} %copy.112, ...), kind=kLoop, calls=%fused_computation.127 | loop fusion | flops 7077888 | bytes 14761984 | tf_op jit(solution)/shard_map/convert_element_type | solution.py:213
  714.4 5.5 copy.111
  724.2 5.5 copy.114
  742.7 5.0 fusion.117
  753.6 157.5 %all-reduce.3.cloned.1.call-done = (f32[768,768]{1,0:T(8,128)}, f32[768,768]{1,0:T(8,128)}, f32[768,768]{1,0:T(8,128)}, f32[768,768]{1,0:T(8,128)}) async-done(((f32[768,768]{1,0:T(8,128)}, f32[768,768]{1,0:T(8,128)}, f32[768,768]{1,0:T(8,128)}, f32[768,768]{1,0:T(8,128)}), (f32[768,768]{1,0:T(8,128)}, f32[768,768]{1,0:T(8,128)}, f32[768,768]{1,0:T(8,128)}, ...) | async-done | bytes 9437200 | tf_op jit(solution)/shard_map/psum | solution.py:232
  (605 shorter events, 596.5 us)
Async XLA Ops:
  7.2 23.6 %copy-start = (bf16[1,1024,768]{2,1,0:T(8,128)(2,1)S(1)}, bf16[1,1024,768]{2,1,0:T(8,128)(2,1)}, u32[]{:S(2)}) copy-start(bf16[1,1024,768]{2,1,0:T(8,128)(2,1)} %param.16) | copy-start | bytes 4718596
  36.1 6.4 copy-start.8
  36.1 29.0 %all-to-all-start.1 = ((bf16[8,128,768]{2,1,0:T(8,128)(2,1)}), bf16[8,128,768]{2,1,0:T(8,128)(2,1)}, u32[]{:S(2)}, u32[]{:S(2)}) async-start(bf16[8,128,768]{2,1,0:T(8,128)(2,1)} %broadcast_select_fusion), calls=%async_computation.1 | async-start | bytes 3145728 | tf_op jit(solution)/shard_map/all_to_all | solution.py:137
  40.5 255.1 %all-gather.2.cloned.1.call-start = ((), (), s32[]{:S(2)}) async-start(), calls=%async_computation.3 | async-start | bytes 1769472 | tf_op jit(solution)/shard_map/all_gather | solution.py:14
  64.4 281.8 %copy-start.14 = (pred[1024,16]{1,0:T(8,128)(4,1)}, pred[1024,16]{1,0:T(8,128)(4,1)S(1)}, u32[]{:S(2)}) copy-start(pred[1024,16]{1,0:T(8,128)(4,1)S(1)} %copy.94) | copy-start | bytes 49156
  71.5 3.3 copy-start.10
  132.4 563.3 %reduce-scatter.4.cloned.1.call-start = ((), (), s32[]{:S(2)}) async-start(), calls=%async_computation.4 | async-start | bytes 3538944
  135.9 3.2 copy-start.4
  139.0 3.2 copy-start.28
  139.0 5.3 copy-start.19
  139.0 5.3 copy-start.20
  144.3 142.7 %copy-start.16 = (bf16[64,16,48]{2,1,0:T(8,128)(2,1)S(1)}, bf16[64,16,48]{2,1,0:T(8,128)(2,1)}, u32[]{:S(2)}) copy-start(bf16[64,16,48]{2,1,0:T(8,128)(2,1)} %get-tuple-element.310) | copy-start | bytes 294916
  343.4 2.7 copy-start.25
  346.2 13.4 %copy-start.3 = (bf16[1024,16,48]{2,1,0:T(8,128)(2,1)S(1)}, bf16[1024,16,48]{2,1,0:T(8,128)(2,1)}, u32[]{:S(2)}) copy-start(bf16[1024,16,48]{2,1,0:T(8,128)(2,1)} %copy.100) | copy-start | bytes 4718596
  359.6 3.0 copy-start.22
  474.7 436.5 %all-reduce.3.cloned.1.call-start = ((), (), s32[]{:S(2)}) async-start(), calls=%async_computation.5 | async-start | bytes 18874368 | tf_op jit(solution)/shard_map/psum | solution.py:232
  686.0 5.5 copy-start.9
  714.4 5.5 copy-start.11
  742.7 5.0 copy-start.12
  742.7 5.0 copy-start.29
  911.1 3.4 copy-start.7
  914.5 2.5 copy-start.6
  917.0 2.5 copy-start.5
  917.0 3.9 copy-start.1
  (26 other events, 46.8 us)
Sparse Core Ops, SparseCore 0:
  132.6 52.8 all-gather.1
  474.8 81.6 reduce-scatter.3
  742.8 168.2 all-reduce.2
where the time goes:
time: 942 us; the launch traced here: 928 us
  matrix products  454 us (48%)
  local copies, waits for them, and re-layouts  204 us (22%)
  waiting for transfers between devices  158 us (17%)
  other arithmetic  76.5 us (8%)
  between operations  15.1 us (2%)
  blocking collectives  13.8 us (1%)
    dot_general x224, matrix products, product(): jnp.einsum(pattern, left_side, right_side, preferred_element_type=jnp.flo...  413 us
    psum x1, waiting for transfers between devices, per_device(): lax.psum((grad_query, grad_key, grad_value, grad_outproj), ('seq', 'rep'))  158 us
    while x9, local copies, waits for them, and re-layouts, heads_map(): lax.map(lambda members: function(*members, pieces, scaling), transposed)  35.9 us
    while x32, local copies, waits for them, and re-layouts  30.8 us
    convert_element_type x6, local copies, waits for them, and re-layouts, sparse_rows(): dense.astype(jnp.float32)  30.7 us
    dot_general x8, matrix products, project(): return jnp.dot(left_side, right_side, preferred_element_type=jnp.float32)  24 us
  transfers between devices with their start and end apart: 4, of which 1 were waited for; matrix products, arithmetic and copies ran while one was open for 41% of the time, Pallas kernels for 0%

commit v1 on v0

--- a/solution.py
+++ b/solution.py
@@ -229,7 +229,9 @@
     grad_query = jnp.einsum("td,te->de", embedded, query_grad, preferred_element_type=jnp.float32)
     grad_key = jnp.einsum("td,te->de", embedded, key_grad, preferred_element_type=jnp.float32)
     grad_value = jnp.einsum("td,te->de", embedded, value_grad, preferred_element_type=jnp.float32)
-    summed = lax.psum((grad_query, grad_key, grad_value, grad_outproj), ("seq", "rep"))
+    summed = (grad_query, grad_key, grad_value, grad_outproj)
+    for over in ("rep", "seq"):
+        summed = lax.psum(summed, over)
     return (encoded[None], embed_grad[None], summed[0], summed[1], summed[2], summed[3])
 
 

time: 942 us -> 1310 us (1.39)
  waiting for transfers between devices: 158 us -> 526 us
    psum x1 -> x2, waiting for transfers between devices: 158 us -> 526 us  [per_device(): summed = lax.psum(summed, over)]
  transfers between devices with their start and end apart: 4 -> 5, of which waited for: 1 -> 2; matrix products, arithmetic and copies ran while one was open for 41% -> 30% of each run, Pallas kernels for 0% -> 0%
where the time goes in v1:
time: 1310 us; the launch traced here: 1300 us
  waiting for transfers between devices  526 us (40%)
  matrix products  453 us (35%)
  local copies, waits for them, and re-layouts  204 us (16%)
  other arithmetic  76.5 us (6%)
  between operations  15.1 us (1%)
  blocking collectives  13.8 us (1%)
    psum x2, waiting for transfers between devices, per_device(): summed = lax.psum(summed, over)  526 us
    dot_general x224, matrix products, product(): jnp.einsum(pattern, left_side, right_side, preferred_element_type=jnp.flo...  413 us
    while x9, local copies, waits for them, and re-layouts, heads_map(): lax.map(lambda members: function(*members, pieces, scaling), transposed)  35.9 us
    while x32, local copies, waits for them, and re-layouts  31 us
    convert_element_type x6, local copies, waits for them, and re-layouts, sparse_rows(): dense.astype(jnp.float32)  30.7 us
  transfers between devices with their start and end apart: 5, of which 2 were waited for; matrix products, arithmetic and copies ran while one was open for 30% of the time, Pallas kernels for 0%

profile of v1, /device:TPU:1, one launch (start us, length us, event | category | flops | bytes accessed | tf_op | source)
XLA Modules:
  0.0 1295.9 jit_solution(10087760105281292511)
XLA Ops:
  16.9 13.8 %all_to_all.14 = s32[8,1,128]{2,1,0:T(1,128)S(1)} all-to-all(s32[8,1,128]{2,1,0:T(1,128)S(1)} %bitcast.386), channel_id=1, replica_groups=mesh['seq'=8,'rep'=16] {'seq'}, dimensions={0} | all-to-all | bytes 8192 | tf_op jit(solution)/shard_map/all_to_all | solution.py:135
  47.3 4.8 copy.100
  55.2 7.8 reshape.434
  65.1 6.4 scatter_custom_fusion
  76.8 7.8 reshape.431
  90.0 7.8 reshape.432
  105.2 7.8 reshape.433
  113.0 14.1 %select_reduce_fusion = (bf16[64,16,48]{2,1,0:T(8,128)(2,1)S(1)}, bf16[64,16,48]{2,1,0:T(8,128)(2,1)}, bf16[64,16,48]{2,1,0:T(8,128)(2,1)}, bf16[64,16,48]{2,1,0:T(8,128)(2,1)}) fusion(f32[64,16,16,48]{3,2,1,0:T(8,128)} %reshape.434, pred[16,16]{1,0:T(8,128)(4,1)} %copy-done.23, f32[64,16,16,48]{3,2,1,0:T(8,128)} %reshape.432, ...), kind=kLoop, calls=%fused_computation.133 | loop fusion | flops 6094848 | bytes 12976384 | tf_op jit(solution)/shard_map/reduce_sum | solution.py:38
  144.3 142.8 %while.56 = (s32[]{:T(128)}, f32[16,1024,48]{1,2,0:T(8,128)}, f32[16,1024]{1,0:T(8,128)S(1)}, f32[16,1024]{1,0:T(8,128)S(1)}, pred[16,1024]{1,0:T(8,128)(4,1)S(1...) while((s32[]{:T(128)}, f32[16,1024,48]{1,2,0:T(8,128)}, ...), condition=%wide.region_5.6_spmd, body=%wide.region_2.5_spmd.sunk | while | flops 212858880 | bytes 30383244 | solution.py:102
  287.2 7.9 copy.83
  301.4 42.2 %while.57 = (s32[]{:T(128)}, f32[16,64,48]{1,2,0:T(8,128)S(1)}, f32[16,64]{1,0:T(8,128)S(1)}, f32[16,64]{1,0:T(8,128)S(1)}, pred[16,512]{1,0:T(8,128)(4,1)S(1)},...) while((s32[]{:T(128)}, f32[16,64,48]{1,2,0:T(8,128)S(1)}, ...), condition=%wide.region_12.13_spmd, body=%wide.region_9.12_spmd.sunk | while | flops 6520706 | bytes 702321 | solution.py:102
  346.3 13.4 %multiply_convert_fusion.1 = (bf16[1024,16,48]{2,1,0:T(8,128)(2,1)}, f32[1024,16,48]{2,1,0:T(8,128)S(1)}) fusion(f32[1024]{0:T(1024)S(1)} %copy-done.25, f32[1024,16]{1,0:T(8,128)} %copy.97, f32[1024,16]{1,0:T(8,128)S(1)} %copy.96, f32[64,16,48]{2,1,0:T(8,128)S(1)} %copy.95, pred[1024,16]{1,0:T(8,128)(4,1)S(1)} %copy.94, f32[1024,16]{1,0:T(8,128)S(1)} %copy.93, ...), kind=kLoop, calls=%fused_computation.135 | loop fusion | flops 5505024 | bytes 8278016 | tf_op jit(solution)/shard_map/convert_element_type | solution.py:172
  363.1 103.9 %while.59 = (s32[]{:T(128)}, f32[16,64,48]{1,2,0:T(8,128)S(1)}, f32[16,512,48]{1,2,0:T(8,128)}, f32[16,512,48]{1,2,0:T(8,128)}, pred[16,512]{1,0:T(8,128)(4,1)S(...) while((s32[]{:T(128)}, f32[16,64,48]{1,2,0:T(8,128)S(1)}, ...), condition=%wide.region_20.21_spmd, body=%wide.region_19.20_spmd.sunk | while | flops 15985666 | bytes 1278077 | solution.py:102
  481.1 181.1 %while.58 = (s32[]{:T(128)}, f32[16,1024,48]{1,2,0:T(8,128)}, f32[16,1024,48]{1,2,0:T(8,128)}, f32[16,1024,48]{1,2,0:T(8,128)}, pred[16,1024]{1,0:T(8,128)(4,1)S...) while((s32[]{:T(128)}, f32[16,1024,48]{1,2,0:T(8,128)}, ...), condition=%wide.region_15.16_spmd, body=%wide.region_14.15_spmd.sunk | while | flops 513900544 | bytes 21337212 | solution.py:102
  662.5 7.9 copy.102
  670.4 7.8 copy.112
  678.2 7.9 copy.115
  686.1 5.5 copy.98
  699.3 15.1 %fusion.110 = (bf16[1024,16,48]{2,1,0:T(8,128)(2,1)}, bf16[1024,16,48]{2,1,0:T(8,128)(2,1)}, bf16[1024,16,48]{2,1,0:T(8,128)(2,1)}) fusion(f32[16,1024,48]{2,0,1:T(8,128)} %copy.102, f32[64,16,48]{2,1,0:T(8,128)S(1)} %copy.110, pred[1024,16]{1,0:T(8,128)(4,1)} %copy-done.14, f32[64,16,48]{2,1,0:T(8,128)S(1)} %copy.113, f32[16,1024,48]{2,0,1:T(8,128)} %copy.112, ...), kind=kLoop, calls=%fused_computation.127 | loop fusion | flops 7077888 | bytes 14761984 | tf_op jit(solution)/shard_map/convert_element_type | solution.py:213
  714.5 5.5 copy.111
  724.2 5.5 copy.114
  742.8 149.1 %all-reduce.5.cloned.1.call-done = (f32[768,768]{1,0:T(8,128)}, f32[768,768]{1,0:T(8,128)}, f32[768,768]{1,0:T(8,128)}, f32[768,768]{1,0:T(8,128)}) async-done(((f32[768,768]{1,0:T(8,128)}, f32[768,768]{1,0:T(8,128)}, f32[768,768]{1,0:T(8,128)}, f32[768,768]{1,0:T(8,128)}), (f32[768,768]{1,0:T(8,128)}, f32[768,768]{1,0:T(8,128)}, f32[768,768]{1,0:T(8,128)}, ...) | async-done | bytes 9437200 | tf_op jit(solution)/shard_map/psum | solution.py:234
  891.9 5.0 fusion.117
  902.7 376.6 %all-reduce.7.cloned.1.call-done = (f32[768,768]{1,0:T(8,128)}, f32[768,768]{1,0:T(8,128)}, f32[768,768]{1,0:T(8,128)}, f32[768,768]{1,0:T(8,128)}) async-done(((f32[768,768]{1,0:T(8,128)}, f32[768,768]{1,0:T(8,128)}, f32[768,768]{1,0:T(8,128)}, f32[768,768]{1,0:T(8,128)}), (f32[768,768]{1,0:T(8,128)}, f32[768,768]{1,0:T(8,128)}, f32[768,768]{1,0:T(8,128)}, ...) | async-done | bytes 9437200 | tf_op jit(solution)/shard_map/psum | solution.py:234
  (608 shorter events, 601.1 us)
Async XLA Ops:
  7.2 23.6 %copy-start = (bf16[1,1024,768]{2,1,0:T(8,128)(2,1)S(1)}, bf16[1,1024,768]{2,1,0:T(8,128)(2,1)}, u32[]{:S(2)}) copy-start(bf16[1,1024,768]{2,1,0:T(8,128)(2,1)} %param.16) | copy-start | bytes 4718596
  36.1 6.4 copy-start.8
  36.1 29.0 %all-to-all-start.1 = ((bf16[8,128,768]{2,1,0:T(8,128)(2,1)}), bf16[8,128,768]{2,1,0:T(8,128)(2,1)}, u32[]{:S(2)}, u32[]{:S(2)}) async-start(bf16[8,128,768]{2,1,0:T(8,128)(2,1)} %broadcast_select_fusion), calls=%async_computation.1 | async-start | bytes 3145728 | tf_op jit(solution)/shard_map/all_to_all | solution.py:137
  40.5 255.2 %all-gather.2.cloned.1.call-start = ((), (), s32[]{:S(2)}) async-start(), calls=%async_computation.3 | async-start | bytes 1769472 | tf_op jit(solution)/shard_map/all_gather | solution.py:14
  64.4 281.9 %copy-start.14 = (pred[1024,16]{1,0:T(8,128)(4,1)}, pred[1024,16]{1,0:T(8,128)(4,1)S(1)}, u32[]{:S(2)}) copy-start(pred[1024,16]{1,0:T(8,128)(4,1)S(1)} %copy.94) | copy-start | bytes 49156
  71.5 3.3 copy-start.10
  132.4 563.3 %reduce-scatter.4.cloned.1.call-start = ((), (), s32[]{:S(2)}) async-start(), calls=%async_computation.4 | async-start | bytes 3538944
  135.9 3.2 copy-start.4
  139.0 3.2 copy-start.28
  139.0 5.2 copy-start.19
  139.0 5.2 copy-start.20
  144.3 142.8 %copy-start.16 = (bf16[64,16,48]{2,1,0:T(8,128)(2,1)S(1)}, bf16[64,16,48]{2,1,0:T(8,128)(2,1)}, u32[]{:S(2)}) copy-start(bf16[64,16,48]{2,1,0:T(8,128)(2,1)} %get-tuple-element.310) | copy-start | bytes 294916
  343.6 2.7 copy-start.25
  346.3 13.4 %copy-start.3 = (bf16[1024,16,48]{2,1,0:T(8,128)(2,1)S(1)}, bf16[1024,16,48]{2,1,0:T(8,128)(2,1)}, u32[]{:S(2)}) copy-start(bf16[1024,16,48]{2,1,0:T(8,128)(2,1)} %copy.100) | copy-start | bytes 4718596
  359.7 3.0 copy-start.22
  474.8 417.1 %all-reduce.5.cloned.1.call-start = ((), (), s32[]{:S(2)}) async-start(), calls=%async_computation.5 | async-start | bytes 18874368 | tf_op jit(solution)/shard_map/psum | solution.py:234
  686.1 5.5 copy-start.9
  714.5 5.5 copy-start.11
  742.7 536.6 %all-reduce.7.cloned.1.call-start = ((), (), s32[]{:S(2)}) async-start(), calls=%async_computation.6 | async-start | bytes 18874368 | tf_op jit(solution)/shard_map/psum | solution.py:234
  891.9 5.0 copy-start.12
  891.9 5.0 copy-start.29
  1279.3 3.4 copy-start.7
  1282.7 2.5 copy-start.6
  1285.2 3.9 copy-start.1
  (27 other events, 49.5 us)
Sparse Core Ops, SparseCore 0:
  132.6 52.8 all-gather.1
  474.9 81.6 reduce-scatter.3
  742.8 148.9 all-reduce.4
  894.4 384.8 all-reduce.6
